TPU v7x, 32 devices: a whole 2x2x4 slice. The times are simulated.
32 devices in a mesh: groups: 2 (over y), ctx: 4 (over z), mp: 2 (over x), rep: 2 (over core).
Axes of the slice: x: 2, y: 2, z: 4, core: 2. Of those that a mesh axis runs over, the one named last changes fastest.
Arguments:
- lru_in: bfloat16 [2048, 4096], P(('groups', 'ctx', 'mp'), 'rep'), parts along dimension 0, may hold values from -6 to 6
- gate_weights: bfloat16 [2, 16, 256, 256], P(None, 'rep', 'mp'), may hold values from -0.375 to 0.375
- decay_param: float32 [4096], P('rep'), may hold values from 4 to 13
- queries: bfloat16 [2048, 2048], P(('groups', 'ctx', 'mp'), 'rep'), parts along dimension 0, may hold values from -7.5 to 7.5
- keys_values: bfloat16 [2048, 256], P(('groups', 'ctx', 'mp')), parts along dimension 0, may hold values from -4 to 4
Outputs:
- recurrent: bfloat16 [2048, 4096], P(('groups', 'ctx', 'mp'), 'rep'), parts along dimension 0
- attended: bfloat16 [2048, 2048], P(('groups', 'ctx', 'mp'), 'rep'), parts along dimension 0
There are 2 independent parts, one for each index of `groups`. A program takes and returns all parts, laid end to end along the dimension named above; an argument that names none is the same for every part. Nothing has to cross between parts.
All inputs are finite; a program needn't handle non-finite values.
Results may differ from a plain program's by a relative error of at most 0.0048.
Values may be sent and summed in bfloat16 or wider, within the bound.
A program may use at most 64 MiB of HBM per device.

v0:
```python
import math

import jax
import jax.numpy as jnp
from jax import lax
from jax.sharding import PartitionSpec as P

WINDOW = 2048


def entering(x, axis, combine, identity):
    length, index = (lax.axis_size(axis), lax.axis_index(axis))
    everything = jax.tree.map(lambda part: lax.all_gather(part, axis), x)
    start = jax.tree.map(
        lambda part, zero: jnp.broadcast_to(jnp.asarray(zero, part.dtype), part.shape), x, identity
    )

    def lap(k, before):
        reached = k < index
        new = combine(before, jax.tree.map(lambda part: part[k], everything))
        return jax.tree.map(lambda a, b: jnp.where(reached, a, b), new, before)

    return lax.fori_loop(0, length, lap, start)


def from_behind(x, axis, by):
    length = lax.axis_size(axis)
    pairs = [(i, i + by) for i in range(length) if 0 <= i + by < length]
    return lax.ppermute(x, axis, pairs)


def pair_combine(first_pair, second_pair):
    return (first_pair[0] * second_pair[0], second_pair[0] * first_pair[1] + second_pair[1])


def prefix_before(all_decay, all_state, limit_count):
    unit_decay = jnp.ones_like(all_decay[0])
    zero_state = jnp.zeros_like(all_state[0])

    def advance(device_index, running):
        active = device_index < limit_count
        decay_next = jnp.where(active, running[0] * all_decay[device_index], running[0])
        state_next = jnp.where(
            active, all_decay[device_index] * running[1] + all_state[device_index], running[1]
        )
        return (decay_next, state_next)

    return lax.fori_loop(0, all_decay.shape[0], advance, (unit_decay, zero_state))


def on_device(lru_in, gate_weights, decay_param, queries, keys_values):
    row_count, local_width = lru_in.shape
    block_count = gate_weights.shape[1]
    block_width = gate_weights.shape[3]
    x_blocks = lru_in.reshape(row_count, block_count, block_width)
    gate_sums = jnp.einsum(
        "tbi,gbio->gtbo",
        x_blocks,
        lax.all_gather(gate_weights, "mp", axis=2, tiled=True),
        preferred_element_type=jnp.float32,
    )
    gate_sums = gate_sums.reshape(2, row_count, local_width)
    decay_rate = jax.nn.softplus(-decay_param)
    log_decay = -8.0 * decay_rate[None, :] * jax.nn.sigmoid(gate_sums[0])
    driven = (
        jnp.sqrt(-jnp.expm1(2.0 * log_decay))
        * jax.nn.sigmoid(gate_sums[1])
        * lru_in.astype(jnp.float32)
    )
    decays = jnp.exp(log_decay)
    run_decay, run_state = lax.associative_scan(pair_combine, (decays, driven), axis=0)
    final_pair = (run_decay[-1], run_state[-1])
    identity = (jnp.ones_like(final_pair[0]), jnp.zeros_like(final_pair[1]))
    member_decay, member_state = (
        lax.all_gather(final_pair[0][None], "mp", axis=0, tiled=True),
        lax.all_gather(final_pair[1][None], "mp", axis=0, tiled=True),
    )
    before = prefix_before(member_decay, member_state, lax.axis_index("mp"))
    totals = prefix_before(member_decay, member_state, lax.axis_size("mp"))
    group_state = entering(totals, "ctx", pair_combine, identity)
    carried = before[0] * group_state[1] + before[1]
    recurrent = (run_state + run_decay * carried[None, :]).astype(jnp.bfloat16)
    head_dim = keys_values.shape[1] // 2
    position = lax.axis_index(("ctx", "mp"))
    needed = WINDOW // row_count
    reach_count = min(needed, lax.axis_size(("ctx", "mp")) - 1)
    earlier = [
        from_behind(keys_values, ("ctx", "mp"), distance) for distance in range(reach_count, 0, -1)
    ]
    missing = jnp.zeros(((needed - reach_count) * row_count, 2 * head_dim), jnp.bfloat16)
    context = jnp.concatenate([missing] + earlier + [keys_values], axis=0)
    key_rows = context[:, :head_dim]
    value_rows = context[:, head_dim:]
    heads_here = queries.shape[1] // head_dim
    score_scale = 1.0 / math.sqrt(head_dim)
    query_pos = position * row_count + jnp.arange(row_count, dtype=jnp.int32)
    key_pos = position * row_count - WINDOW + jnp.arange(WINDOW + row_count, dtype=jnp.int32)
    allowed = (
        (key_pos[None, :] >= 0)
        & (key_pos[None, :] <= query_pos[:, None])
        & (key_pos[None, :] > query_pos[:, None] - WINDOW)
    )
    query_heads = queries.reshape(row_count, heads_here // 2, 2, head_dim).transpose(1, 0, 2, 3)

    def attend_pair(head_pair):
        scores = (
            jnp.einsum("thd,kd->htk", head_pair, key_rows, preferred_element_type=jnp.float32)
            * score_scale
        )
        scores = jnp.where(allowed[None, :, :], scores, jnp.float32(-1e30))
        row_max = jnp.max(scores, axis=2, keepdims=True)
        expd = jnp.exp(scores - row_max)
        probabilities = (expd / jnp.sum(expd, axis=2, keepdims=True)).astype(jnp.bfloat16)
        return jnp.einsum(
            "htk,kd->thd", probabilities, value_rows, preferred_element_type=jnp.float32
        ).astype(jnp.bfloat16)

    attended = lax.map(attend_pair, query_heads)
    attended = attended.transpose(1, 0, 2, 3).reshape(row_count, heads_here * head_dim)
    return (recurrent, attended)


def solution(mesh):
    in_specs = (
        P(("groups", "ctx", "mp"), "rep"),
        P(None, "rep", "mp", None),
        P("rep"),
        P(("groups", "ctx", "mp"), "rep"),
        P(("groups", "ctx", "mp"), None),
    )
    out_specs = (P(("groups", "ctx", "mp"), "rep"), P(("groups", "ctx", "mp"), "rep"))
    return jax.shard_map(
        on_device, mesh=mesh, in_specs=in_specs, out_specs=out_specs, check_vma=False
    )
```

profile of v0, /device:TPU:0, one launch (start us, length us, event | category | flops | bytes accessed | tf_op | source)
XLA Modules:
  0.0 137.2 jit_solution(17895876114866354596)
XLA Ops:
  7.2 5.0 %collective-permute-start.5 = (bf16[128,256]{1,0:T(8,128)(2,1)}, bf16[128,256]{1,0:T(8,128)(2,1)S(1)}, u32[]{:S(2)}, u32[]{:S(2)}) collective-permute-start(bf16[128,256]{1,0:T(8,128)(2,1)} %param.17), channel_id=1, source_target_pairs={{0,4},{2,6},{4,8},{6,10},{8,12},{10,14},{1,5},{3,7},{5,9},{7,11},{... | collective-permute-start | bytes 196616 | tf_op jit(solution)/shard_map/ppermute | solution.py:29
  12.2 4.4 %collective-permute-start.4 = (bf16[128,256]{1,0:T(8,128)(2,1)}, bf16[128,256]{1,0:T(8,128)(2,1)S(1)}, u32[]{:S(2)}, u32[]{:S(2)}) collective-permute-start(bf16[128,256]{1,0:T(8,128)(2,1)} %param.17), channel_id=1, source_target_pairs={{0,6},{2,8},{4,10},{6,12},{8,14},{1,7},{3,9},{5,11},{7,13},{9,15},... | collective-permute-start | bytes 196616 | tf_op jit(solution)/shard_map/ppermute | solution.py:29
  16.6 2.3 %collective-permute-start.3 = (bf16[128,256]{1,0:T(8,128)(2,1)}, bf16[128,256]{1,0:T(8,128)(2,1)S(1)}, u32[]{:S(2)}, u32[]{:S(2)}) collective-permute-start(bf16[128,256]{1,0:T(8,128)(2,1)} %param.17), channel_id=1, source_target_pairs={{0,8},{2,10},{4,12},{6,14},{1,9},{3,11},{5,13},{7,15},{16,24},{18,... | collective-permute-start | bytes 196616 | tf_op jit(solution)/shard_map/ppermute | solution.py:29
  21.5 2.3 %copy.19 = bf16[2,8,128,256]{2,3,0,1:T(8,128)(2,1)} copy(bf16[2,8,128,256]{3,2,1,0:T(8,128)(2,1)} %param.14) | data formatting | bytes 2097152 | tf_op args[1]
  29.0 6.1 %collective-permute-start.6 = (bf16[128,256]{1,0:T(8,128)(2,1)S(1)}, bf16[128,256]{1,0:T(8,128)(2,1)S(1)}, u32[]{:S(2)}, u32[]{:S(2)}) collective-permute-start(bf16[128,256]{1,0:T(8,128)(2,1)S(1)} %copy-done.4), channel_id=1, source_target_pairs={{0,2},{2,4},{4,6},{6,8},{8,10},{10,12},{12,14},{1,3},{3,5},{5,7},{... | collective-permute-start | bytes 196616 | tf_op jit(solution)/shard_map/ppermute | solution.py:29
  35.2 3.2 %collective-permute-done.6 = bf16[128,256]{1,0:T(8,128)(2,1)S(1)} collective-permute-done((bf16[128,256]{1,0:T(8,128)(2,1)S(1)}, bf16[128,256]{1,0:T(8,128)(2,1)S(1)}, u32[]{:S(2)}, u32[]{:S(2)}) %collective-permute-start.6) | collective-permute-done | bytes 65568 | tf_op jit(solution)/shard_map/ppermute | solution.py:29
  38.5 25.6 %while.57 = (s32[]{:T(128)}, bf16[4,128,2,128]{3,1,2,0:T(8,128)(2,1)}, bf16[4,128,2,128]{1,3,2,0:T(8,128)(2,1)}, bf16[2176,128]{1,0:T(8,128)(2,1)S(1)}, bf16[217...) while((s32[]{:T(128)}, ...), condition=%wide.region_9.10_spmd.clone, body=%wide.region_6.9_spmd.clone.sunk | while | flops 289704064 | bytes 6272757 | solution.py:118
  38.9 3.3 %fusion.64 = (f32[2,128]{1,0:T(2,128)S(1)}, f32[2,128,2176]{2,1,0:T(8,128)}) fusion(pred[128,2176]{1,0:T(8,128)(4,1)S(1)} %compare_and_fusion.2, bf16[2176,128]{1,0:T(8,128)(2,1)S(1)} %get-tuple-element.809, bf16[4,128,2,128]{1,3,2,0:T(8,128)(2,1)} %get-tuple-element.808, s32[]{:T(128)S(6)} %copy.74), kind=kOutput, calls=%fused_computation.114.clone.1 | convolution fusion | flops 144836736 | bytes 3130372 | tf_op jit(solution)/shard_map/while/body/eval_jaxpr/sub | solution.py:112
  42.2 2.8 %fusion.65 = bf16[4,128,2,128]{3,1,2,0:T(8,128)(2,1)} fusion(bf16[4,128,2,128]{3,1,2,0:T(8,128)(2,1)} %get-tuple-element.797, s32[]{:T(128)S(6)} %copy.74, f32[2,128,2176]{2,1,0:T(8,128)} %get-tuple-element.692, f32[2,128]{1,0:T(2,128)S(1)} %get-tuple-element.693, bf16[2176,128]{1,0:T(8,128)(2,1)S(1)} %get-tuple-element.810), kind=kOutput, calls=%fused_computation.10.clone.1 | convolution fusion | flops 143753216 | bytes 2851844 | tf_op jit(solution)/shard_map/while/body/eval_jaxpr/htk,kd->thd/dot_general | solution.py:114
  45.3 3.3 %fusion.64 = (f32[2,128]{1,0:T(2,128)S(1)}, f32[2,128,2176]{2,1,0:T(8,128)}) fusion(pred[128,2176]{1,0:T(8,128)(4,1)S(1)} %compare_and_fusion.2, bf16[2176,128]{1,0:T(8,128)(2,1)S(1)} %get-tuple-element.809, bf16[4,128,2,128]{1,3,2,0:T(8,128)(2,1)} %get-tuple-element.808, s32[]{:T(128)S(6)} %copy.74), kind=kOutput, calls=%fused_computation.114.clone.1 | convolution fusion | flops 144836736 | bytes 3130372 | tf_op jit(solution)/shard_map/while/body/eval_jaxpr/sub | solution.py:112
  48.6 2.8 %fusion.65 = bf16[4,128,2,128]{3,1,2,0:T(8,128)(2,1)} fusion(bf16[4,128,2,128]{3,1,2,0:T(8,128)(2,1)} %get-tuple-element.797, s32[]{:T(128)S(6)} %copy.74, f32[2,128,2176]{2,1,0:T(8,128)} %get-tuple-element.692, f32[2,128]{1,0:T(2,128)S(1)} %get-tuple-element.693, bf16[2176,128]{1,0:T(8,128)(2,1)S(1)} %get-tuple-element.810), kind=kOutput, calls=%fused_computation.10.clone.1 | convolution fusion | flops 143753216 | bytes 2851844 | tf_op jit(solution)/shard_map/while/body/eval_jaxpr/htk,kd->thd/dot_general | solution.py:114
  51.7 3.3 %fusion.64 = (f32[2,128]{1,0:T(2,128)S(1)}, f32[2,128,2176]{2,1,0:T(8,128)}) fusion(pred[128,2176]{1,0:T(8,128)(4,1)S(1)} %compare_and_fusion.2, bf16[2176,128]{1,0:T(8,128)(2,1)S(1)} %get-tuple-element.809, bf16[4,128,2,128]{1,3,2,0:T(8,128)(2,1)} %get-tuple-element.808, s32[]{:T(128)S(6)} %copy.74), kind=kOutput, calls=%fused_computation.114.clone.1 | convolution fusion | flops 144836736 | bytes 3130372 | tf_op jit(solution)/shard_map/while/body/eval_jaxpr/sub | solution.py:112
  55.0 2.8 %fusion.65 = bf16[4,128,2,128]{3,1,2,0:T(8,128)(2,1)} fusion(bf16[4,128,2,128]{3,1,2,0:T(8,128)(2,1)} %get-tuple-element.797, s32[]{:T(128)S(6)} %copy.74, f32[2,128,2176]{2,1,0:T(8,128)} %get-tuple-element.692, f32[2,128]{1,0:T(2,128)S(1)} %get-tuple-element.693, bf16[2176,128]{1,0:T(8,128)(2,1)S(1)} %get-tuple-element.810), kind=kOutput, calls=%fused_computation.10.clone.1 | convolution fusion | flops 143753216 | bytes 2851844 | tf_op jit(solution)/shard_map/while/body/eval_jaxpr/htk,kd->thd/dot_general | solution.py:114
  58.1 3.3 %fusion.64 = (f32[2,128]{1,0:T(2,128)S(1)}, f32[2,128,2176]{2,1,0:T(8,128)}) fusion(pred[128,2176]{1,0:T(8,128)(4,1)S(1)} %compare_and_fusion.2, bf16[2176,128]{1,0:T(8,128)(2,1)S(1)} %get-tuple-element.809, bf16[4,128,2,128]{1,3,2,0:T(8,128)(2,1)} %get-tuple-element.808, s32[]{:T(128)S(6)} %copy.74), kind=kOutput, calls=%fused_computation.114.clone.1 | convolution fusion | flops 144836736 | bytes 3130372 | tf_op jit(solution)/shard_map/while/body/eval_jaxpr/sub | solution.py:112
  61.4 2.8 %fusion.65 = bf16[4,128,2,128]{3,1,2,0:T(8,128)(2,1)} fusion(bf16[4,128,2,128]{3,1,2,0:T(8,128)(2,1)} %get-tuple-element.797, s32[]{:T(128)S(6)} %copy.74, f32[2,128,2176]{2,1,0:T(8,128)} %get-tuple-element.692, f32[2,128]{1,0:T(2,128)S(1)} %get-tuple-element.693, bf16[2176,128]{1,0:T(8,128)(2,1)S(1)} %get-tuple-element.810), kind=kOutput, calls=%fused_computation.10.clone.1 | convolution fusion | flops 143753216 | bytes 2851844 | tf_op jit(solution)/shard_map/while/body/eval_jaxpr/htk,kd->thd/dot_general | solution.py:114
  66.2 2.3 %convolution_bitcast_fusion = f32[2,128,8,256]{1,3,0,2:T(8,128)S(1)} fusion(bf16[2,8,256,256]{2,3,0,1:T(8,128)(2,1)} %all-gather.6.cloned.1.call-done, bf16[128,8,256,1]{2,1,0,3:T(8,128)(2,1)S(1)} %bitcast.91), kind=kOutput, calls=%fused_computation.35 | convolution fusion | flops 268435456 | bytes 4718592 | tf_op jit(solution)/shard_map/tbi,gbio->gtbo/dot_general | solution.py:56
  70.8 2.2 %convert_multiply_fusion = (f32[128,2048]{1,0:T(8,128)S(1)}, f32[128,2048]{1,0:T(8,128)S(1)}) fusion(bf16[128,2048]{1,0:T(8,128)(2,1)} %param.13, f32[128,2048]{1,0:T(8,128)S(1)} %copy.22, f32[128,2048]{1,0:T(8,128)} %copy.21, f32[2048]{0:T(1024)S(1)} %fusion.46), kind=kLoop, calls=%fused_computation.45 | loop fusion | flops 1572864 | bytes 4726784 | tf_op jit(solution)/shard_map/mul | solution.py:66
  84.0 2.1 %pad.99 = f32[128,2048]{1,0:T(8,128)S(1)} pad(f32[64,2048]{1,0:T(8,128)} %add.303, f32[]{:T(128)} %constant.108.clone.1), padding=1_0_1x0_0_0 | pad | bytes 1572868 | tf_op jit(solution)/shard_map/pad | solution.py:71
  86.1 4.8 %all-gather.3 = f32[2,1,2048]{2,1,0:T(1,128)S(1)} all-gather(f32[1,1,2048]{2,1,0:T(1,128)S(1)} %add_bitcast_fusion), channel_id=1, replica_groups=mesh['groups'=2,'ctx'=4,'mp'=2,'rep'=2] {'mp'}, dimensions={0}, use_global_device_ids=true | all-gather | bytes 24576 | tf_op jit(solution)/shard_map/all_gather | solution.py:76
  91.0 4.6 %pad.113 = f32[128,2048]{1,0:T(8,128)} pad(f32[64,2048]{1,0:T(8,128)} %add.311, f32[]{:T(128)} %constant.108.clone.1), padding=1_0_1x0_0_0 | pad | bytes 1572868 | tf_op jit(solution)/shard_map/pad | solution.py:71
  96.4 4.4 %all-gather.2 = f32[2,1,2048]{2,1,0:T(1,128)S(1)} all-gather(f32[1,1,2048]{2,1,0:T(1,128)S(1)} %add_bitcast_fusion.1), channel_id=1, replica_groups=mesh['groups'=2,'ctx'=4,'mp'=2,'rep'=2] {'mp'}, dimensions={0}, use_global_device_ids=true | all-gather | bytes 24576 | tf_op jit(solution)/shard_map/all_gather | solution.py:75
  101.1 13.5 %all-gather.1 = f32[8192]{0:T(1024)S(1)} all-gather(f32[2048]{0:T(1024)S(1)} %get-tuple-element.335), channel_id=3, replica_groups=mesh['groups'=2,'ctx'=4,'mp'=2,'rep'=2] {'ctx'}, dimensions={0}, use_global_device_ids=true | all-gather | bytes 40960 | tf_op jit(solution)/shard_map/all_gather | solution.py:13
  114.6 13.1 %all-gather = f32[8192]{0:T(1024)S(1)} all-gather(f32[2048]{0:T(1024)S(1)} %get-tuple-element.334), channel_id=2, replica_groups=mesh['groups'=2,'ctx'=4,'mp'=2,'rep'=2] {'ctx'}, dimensions={0}, use_global_device_ids=true | all-gather | bytes 40960 | tf_op jit(solution)/shard_map/all_gather | solution.py:13
  128.0 2.3 %add_convert_fusion = bf16[128,2048]{1,0:T(8,128)(2,1)} fusion(f32[128,2048]{1,0:T(8,128)S(1)} %pad.112, f32[128,2048]{1,0:T(8,128)} %pad.113, f32[128,2048]{1,0:T(8,128)S(1)} %pad.98, f32[128,2048]{1,0:T(8,128)S(1)} %pad.99, f32[2048]{0:T(1024)S(1)} %multiply_add_fusion.6), kind=kLoop, calls=%fused_computation.44 | loop fusion | flops 1310720 | bytes 4726784 | tf_op jit(solution)/shard_map/convert_element_type | solution.py:82
  (182 shorter events, 25.6 us)
Async XLA Ops:
  7.2 59.1 %all-gather.6.cloned.1.call-start = ((), (), s32[]{:S(2)}) async-start(), calls=%async_computation | async-start | bytes 3145728 | tf_op jit(solution)/shard_map/all_gather | solution.py:59
  7.2 28.0 %collective-permute-start.5 = (bf16[128,256]{1,0:T(8,128)(2,1)}, bf16[128,256]{1,0:T(8,128)(2,1)S(1)}, u32[]{:S(2)}, u32[]{:S(2)}) collective-permute-start(bf16[128,256]{1,0:T(8,128)(2,1)} %param.17), channel_id=1, source_target_pairs={{0,4},{2,6},{4,8},{6,10},{8,12},{10,14},{1,5},{3,7},{5,9},{7,11},{... | collective-permute-start | bytes 196616 | tf_op jit(solution)/shard_map/ppermute | solution.py:29
  12.2 23.0 %collective-permute-start.4 = (bf16[128,256]{1,0:T(8,128)(2,1)}, bf16[128,256]{1,0:T(8,128)(2,1)S(1)}, u32[]{:S(2)}, u32[]{:S(2)}) collective-permute-start(bf16[128,256]{1,0:T(8,128)(2,1)} %param.17), channel_id=1, source_target_pairs={{0,6},{2,8},{4,10},{6,12},{8,14},{1,7},{3,9},{5,11},{7,13},{9,15},... | collective-permute-start | bytes 196616 | tf_op jit(solution)/shard_map/ppermute | solution.py:29
  16.6 18.6 %collective-permute-start.3 = (bf16[128,256]{1,0:T(8,128)(2,1)}, bf16[128,256]{1,0:T(8,128)(2,1)S(1)}, u32[]{:S(2)}, u32[]{:S(2)}) collective-permute-start(bf16[128,256]{1,0:T(8,128)(2,1)} %param.17), channel_id=1, source_target_pairs={{0,8},{2,10},{4,12},{6,14},{1,9},{3,11},{5,13},{7,15},{16,24},{18,... | collective-permute-start | bytes 196616 | tf_op jit(solution)/shard_map/ppermute | solution.py:29
  18.9 16.2 %collective-permute-start.2 = (bf16[128,256]{1,0:T(8,128)(2,1)}, bf16[128,256]{1,0:T(8,128)(2,1)S(1)}, u32[]{:S(2)}, u32[]{:S(2)}) collective-permute-start(bf16[128,256]{1,0:T(8,128)(2,1)} %param.17), channel_id=1, source_target_pairs={{0,10},{2,12},{4,14},{1,11},{3,13},{5,15},{16,26},{18,28},{20,30},... | collective-permute-start | bytes 196616 | tf_op jit(solution)/shard_map/ppermute | solution.py:29
  20.2 5.6 %collective-permute-start = (bf16[128,256]{1,0:T(8,128)(2,1)}, bf16[128,256]{1,0:T(8,128)(2,1)S(1)}, u32[]{:S(2)}, u32[]{:S(2)}) collective-permute-start(bf16[128,256]{1,0:T(8,128)(2,1)} %param.17), channel_id=1, source_target_pairs={{0,14},{1,15},{16,30},{17,31}} | collective-permute-start | bytes 196616 | tf_op jit(solution)/shard_map/ppermute | solution.py:29
  23.8 0.7 copy-start.5
  23.8 1.0 copy-start.3
  23.8 1.8 %copy-start = (bf16[128,2048]{1,0:T(8,128)(2,1)S(1)}, bf16[128,2048]{1,0:T(8,128)(2,1)}, u32[]{:S(2)}) copy-start(bf16[128,2048]{1,0:T(8,128)(2,1)} %param.13) | copy-start | bytes 1572868
  23.9 1.9 %copy-start.4 = (bf16[128,256]{1,0:T(8,128)(2,1)S(1)}, bf16[128,256]{1,0:T(8,128)(2,1)}, u32[]{:S(2)}) copy-start(bf16[128,256]{1,0:T(8,128)(2,1)} %param.17) | copy-start | bytes 196612
  25.8 3.2 %collective-permute-start.1 = (bf16[128,256]{1,0:T(8,128)(2,1)S(1)}, bf16[128,256]{1,0:T(8,128)(2,1)S(1)}, u32[]{:S(2)}, u32[]{:S(2)}) collective-permute-start(bf16[128,256]{1,0:T(8,128)(2,1)S(1)} %copy-done.4), channel_id=1, source_target_pairs={{0,12},{2,14},{1,13},{3,15},{16,28},{18,30},{17,29},{19,31}} | collective-permute-start | bytes 196616 | tf_op jit(solution)/shard_map/ppermute | solution.py:29
  29.0 9.4 %collective-permute-start.6 = (bf16[128,256]{1,0:T(8,128)(2,1)S(1)}, bf16[128,256]{1,0:T(8,128)(2,1)S(1)}, u32[]{:S(2)}, u32[]{:S(2)}) collective-permute-start(bf16[128,256]{1,0:T(8,128)(2,1)S(1)} %copy-done.4), channel_id=1, source_target_pairs={{0,2},{2,4},{4,6},{6,8},{8,10},{10,12},{12,14},{1,3},{3,5},{5,7},{... | collective-permute-start | bytes 196616 | tf_op jit(solution)/shard_map/ppermute | solution.py:29
  82.0 1.2 copy-start.1
  82.0 1.4 %copy-start.2 = (f32[63,2048]{1,0:T(8,128)S(1)}, f32[63,2048]{1,0:T(8,128)}, u32[]{:S(2)}) copy-start(f32[63,2048]{1,0:T(8,128)} %slice.223) | copy-start | bytes 1548292
Sparse Core Ops, SparseCore 0:
  24.0 30.3 all-gather.5
where the time goes:
time: 138 us; the launch traced here: 137 us
  blocking collectives  35.8 us (26%)
  matrix products  26.4 us (19%)
  local copies, waits for them, and re-layouts  22.3 us (16%)
  starting transfers between devices  21.7 us (16%)
  between operations  15 us (11%)
  other arithmetic  10.5 us (8%)
  waiting for transfers between devices  5.08 us (4%)
    all_gather x2, blocking collectives, entering(): everything = jax.tree.map(lambda part: lax.all_gather(part, axis), x)  26.6 us
    ppermute x7, starting transfers between devices, from_behind(): return lax.ppermute(x, axis, pairs)  21.7 us
    sub x4, matrix products, attend_pair(): expd = jnp.exp(scores - row_max)  13.1 us
    dot_general x4, matrix products, attend_pair(): jnp.einsum('htk,kd->thd', probabilities, value_rows, preferred_element_ty...  11.1 us
    pad x24, local copies, waits for them, and re-layouts, on_device(): lax.associative_scan(pair_combine, (decays, driven), axis=0)  7.74 us
    slice x44, local copies, waits for them, and re-layouts, on_device(): lax.associative_scan(pair_combine, (decays, driven), axis=0)  5.93 us
    ppermute x7, waiting for transfers between devices, from_behind(): return lax.ppermute(x, axis, pairs)  5.06 us
    all_gather x1, blocking collectives, on_device(): lax.all_gather(final_pair[1][None], 'mp', axis=0, tiled=True)  4.8 us
  transfers between devices with their start and end apart: 8, of which 2 were waited for; matrix products, arithmetic and copies ran while one was open for 23% of the time, Pallas kernels for 0%

commit v1 on v0

v1 whole, which is shorter than its diff:
```python
import functools
import math

import jax
import jax.numpy as jnp
from jax import lax
from jax.experimental import pallas as pl
from jax.experimental.pallas import tpu as pltpu
from jax.sharding import PartitionSpec as P

WINDOW = 2048
MESH = pl.DeviceIdType.MESH
F32 = jnp.float32
BF16 = jnp.bfloat16


def kernel(
    sizes,
    x_hbm, w_hbm, decay_ref, q_hbm, kv_hbm,
    rec_ref, att_ref,
    x_ref, wbuf, q_ref, kvbuf, bias, rate, decay_run, state_run, total, totals_in,
    local_sem, kv_send, kv_recv, w_send, w_recv, f_send, f_recv, t_send, t_recv,
):
    G, C, M = sizes
    length = C * M
    rows, width = x_ref.shape
    blocks, bw = wbuf.shape[1], wbuf.shape[4]
    share = blocks // G
    slots = kvbuf.shape[0]
    hd = kvbuf.shape[2] // 2
    heads = q_ref.shape[1] // hd
    g, c, m, r = (lax.axis_index(n) for n in ("groups", "ctx", "mp", "rep"))
    place = c * M + m

    def at(position):
        return (g, position // M, position % M, r)

    loads = [
        pltpu.make_async_copy(kv_hbm, kvbuf.at[0], local_sem.at[0]),
        pltpu.make_async_copy(x_hbm, x_ref, local_sem.at[1]),
        pltpu.make_async_copy(w_hbm, wbuf.at[:, :, m], local_sem.at[2]),
        pltpu.make_async_copy(q_hbm, q_ref, local_sem.at[3]),
    ]
    for load in loads:
        load.start()

    barrier = pltpu.get_barrier_semaphore()

    def greet(d, _):
        pl.semaphore_signal(barrier, inc=1, device_id=at((place + d) % length), device_id_type=MESH)
        return 0

    lax.fori_loop(1, length, greet, 0)
    for d in range(1, G):
        pl.semaphore_signal(barrier, inc=1, device_id=((g + d) % G, c, m, r), device_id_type=MESH)
    pl.semaphore_wait(barrier, length - 1 + G - 1)

    def kv_copy(d):
        return pltpu.make_async_remote_copy(
            src_ref=kv_hbm, dst_ref=kvbuf.at[d],
            send_sem=kv_send.at[d - 1], recv_sem=kv_recv.at[d - 1],
            device_id=at((place + d) % length), device_id_type=MESH,
        )

    def w_copy(d, k):
        b = g * share + k
        return pltpu.make_async_remote_copy(
            src_ref=w_hbm.at[:, b], dst_ref=wbuf.at[:, b, m],
            send_sem=w_send.at[d - 1, k], recv_sem=w_recv.at[d - 1, k],
            device_id=(g, c, (m + d) % M, r), device_id_type=MESH,
        )

    def f_copy(e, d, k):
        b = g * share + k
        piece = wbuf.at[:, b, (m + M - d) % M]
        return pltpu.make_async_remote_copy(
            src_ref=piece, dst_ref=piece,
            send_sem=f_send.at[e - 1, d - 1, k], recv_sem=f_recv.at[e - 1, d - 1, k],
            device_id=((g + e) % G, c, m, r), device_id_type=MESH,
        )

    def f_arrival(e, d, k):
        b = ((g + G - e) % G) * share + k
        piece = wbuf.at[:, b, (m + M - d) % M]
        return pltpu.make_async_remote_copy(
            src_ref=piece, dst_ref=piece,
            send_sem=f_send.at[e - 1, d - 1, k], recv_sem=f_recv.at[e - 1, d - 1, k],
            device_id=((g + e) % G, c, m, r), device_id_type=MESH,
        )

    def w_arrival(d, k):
        b = g * share + k
        return pltpu.make_async_remote_copy(
            src_ref=w_hbm.at[:, b], dst_ref=wbuf.at[:, b, (m + M - d) % M],
            send_sem=w_send.at[d - 1, k], recv_sem=w_recv.at[d - 1, k],
            device_id=(g, c, (m + d) % M, r), device_id_type=MESH,
        )

    for d in range(1, M):
        w_copy(d, 0).start()
    for d in range(1, slots):
        kv_copy(d).start()
    for k in range(1, share):
        for d in range(1, M):
            w_copy(d, k).start()

    e = jnp.exp(-decay_ref[...])
    s = e / (2.0 + e)
    s2 = s * s
    rate[...] = -16.0 * s * (1.0 + s2 * (1.0 / 3.0 + s2 * (1.0 / 5.0)))

    row = lax.broadcasted_iota(jnp.int32, (rows, rows), 0)
    col = lax.broadcasted_iota(jnp.int32, (rows, rows), 1)
    for d in range(slots):
        back = row - col + d * rows
        allowed = (back >= 0) & (back < WINDOW) & (place >= d)
        bias[:, d * rows : (d + 1) * rows] = jnp.where(allowed, 0.0, -1e30).astype(F32)

    groups8 = rows // 8
    sub = lax.broadcasted_iota(jnp.int32, (groups8, 8, bw), 1)

    def gates(b):
        lanes = pl.ds(pl.multiple_of(b * bw, bw), bw)
        xb = x_ref[:, lanes]
        g0 = jnp.dot(xb, wbuf[0, b].reshape(bw, bw), preferred_element_type=F32)
        g1 = jnp.dot(xb, wbuf[1, b].reshape(bw, bw), preferred_element_type=F32)
        y = rate[:, lanes] * jax.nn.sigmoid(g0)
        poly = 1.0 + y * (1 / 2 + y * (1 / 6 + y * (1 / 24 + y * (1 / 120 + y * (1 / 720)))))
        u = y * poly
        a = (1.0 + u).reshape(groups8, 8, bw)
        v = jnp.sqrt(-u * (2.0 + u)) * jax.nn.sigmoid(g1) * xb.astype(F32)
        v = v.reshape(groups8, 8, bw)
        for shift in (1, 2, 4):
            keep = sub >= shift
            before_v = jnp.where(keep, pltpu.roll(v, shift, 1), 0.0)
            before_a = jnp.where(keep, pltpu.roll(a, shift, 1), 1.0)
            v = a * before_v + v
            a = a * before_a
        decay_run[:, lanes] = a.reshape(rows, bw)
        state_run[:, lanes] = v.reshape(rows, bw)
        ta, tv = a[0, 7:8], v[0, 7:8]
        for k in range(1, groups8):
            tv = a[k, 7:8] * tv + v[k, 7:8]
            ta = a[k, 7:8] * ta
        total[0:1, lanes] = ta
        total[1:2, lanes] = tv

    scale = 1.0 / math.sqrt(hd)

    def head(h):
        lanes = pl.ds(pl.multiple_of(h * hd, hd), hd)
        keys = kvbuf[:, :, :hd].reshape(slots * rows, hd)
        values = kvbuf[:, :, hd:].reshape(slots * rows, hd)
        scores = lax.dot_general(
            q_ref[:, lanes], keys, (((1,), (1,)), ((), ())), preferred_element_type=F32
        )
        scores = scores * scale + bias[...]
        top = jnp.max(scores, axis=1, keepdims=True)
        weights = jnp.exp(scores - top)
        norm = jnp.sum(weights, axis=1, keepdims=True)
        out = jnp.dot(weights.astype(BF16), values, preferred_element_type=F32)
        att_ref[:, lanes] = (out / norm).astype(BF16)

    loads[1].wait()
    loads[2].wait()

    def direct(k, _):
        for d in range(1, M):
            w_arrival(d, k).wait_recv()
            for e in range(1, G):
                f_copy(e, d, k).start()
        gates(g * share + k)
        return 0

    lax.fori_loop(0, share, direct, 0)

    loads[0].wait()
    loads[3].wait()
    for d in range(1, slots):
        kv_copy(d).wait_recv()

    stages = share * (G - 1)
    early = min(heads // 2, stages)

    def early_head(h, _):
        head(h)
        return 0

    for e in range(1, G):
        def relayed(k, _, e=e):
            stage = (e - 1) * share + k

            @pl.when(stage < early)
            def _():
                head(stage)

            for d in range(1, M):
                f_arrival(e, d, k).wait_recv()
            gates(((g + G - e) % G) * share + k)
            return 0

        lax.fori_loop(0, share, relayed, 0)

    def t_copy(d):
        return pltpu.make_async_remote_copy(
            src_ref=total, dst_ref=totals_in.at[d - 1],
            send_sem=t_send.at[d - 1], recv_sem=t_recv.at[d - 1],
            device_id=at((place + d) % length), device_id_type=MESH,
        )

    def t_start(d, _):
        t_copy(d).start()
        return 0

    lax.fori_loop(1, length, t_start, 0)
    lax.fori_loop(early, heads, early_head, 0)

    def t_fold(i, entering):
        d = length - 1 - i
        t_copy(d).wait_recv()
        new = totals_in[d - 1, 0:1] * entering + totals_in[d - 1, 1:2]
        return jnp.where(place >= d, new, entering)

    entering = lax.fori_loop(0, length - 1, t_fold, jnp.zeros((1, width), F32))

    def finish(k, entering):
        pieces = []
        for half in range(2):
            here = pl.ds(pl.multiple_of(k * 16 + half * 8, 8), 8)
            state = state_run[here] + decay_run[here] * entering
            entering = state[7:8]
            pieces.append(state)
        rec_ref[pl.ds(pl.multiple_of(k * 16, 16), 16)] = jnp.concatenate(pieces, axis=0).astype(BF16)
        return entering

    lax.fori_loop(0, rows // 16, finish, entering)

    for d in range(1, slots):
        kv_copy(d).wait_send()

    def w_sent(k, _):
        for d in range(1, M):
            w_copy(d, k).wait_send()
            for e in range(1, G):
                f_copy(e, d, k).wait_send()
        return 0

    lax.fori_loop(0, share, w_sent, 0)

    def t_sent(d, _):
        t_copy(d).wait_send()
        return 0

    lax.fori_loop(1, length, t_sent, 0)


def on_device(lru_in, gate_weights, decay_param, queries, keys_values):
    G, C, M = (lax.axis_size(n) for n in ("groups", "ctx", "mp"))
    length = C * M
    rows, width = lru_in.shape
    _, blocks, depth, bw = gate_weights.shape
    share = blocks // G
    reach = min(WINDOW // rows, length - 1)
    slots = reach + 1
    dma = pltpu.SemaphoreType.DMA
    anywhere = pl.BlockSpec(memory_space=pl.ANY)
    vmem = pl.BlockSpec(memory_space=pltpu.VMEM)
    return pl.pallas_call(
        functools.partial(kernel, (G, C, M)),
        out_shape=(
            jax.ShapeDtypeStruct(lru_in.shape, BF16),
            jax.ShapeDtypeStruct(queries.shape, BF16),
        ),
        in_specs=[anywhere, anywhere, vmem, anywhere, anywhere],
        out_specs=(vmem, vmem),
        scratch_shapes=[
            pltpu.VMEM((rows, width), BF16),
            pltpu.VMEM((2, blocks, M, depth, bw), BF16),
            pltpu.VMEM(queries.shape, BF16),
            pltpu.VMEM((slots,) + keys_values.shape, BF16),
            pltpu.VMEM((rows, slots * rows), F32),
            pltpu.VMEM((1, width), F32),
            pltpu.VMEM((rows, width), F32),
            pltpu.VMEM((rows, width), F32),
            pltpu.VMEM((2, width), F32),
            pltpu.VMEM((length - 1, 2, width), F32),
            dma((4,)),
            dma((reach,)),
            dma((reach,)),
            dma((M - 1, share)),
            dma((M - 1, share)),
            dma((G - 1, M - 1, share)),
            dma((G - 1, M - 1, share)),
            dma((length - 1,)),
            dma((length - 1,)),
        ],
        compiler_params=pltpu.CompilerParams(
            collective_id=0, has_side_effects=True, vmem_limit_bytes=48 * 2**20
        ),
    )(lru_in, gate_weights, decay_param.reshape(1, width), queries, keys_values)


def solution(mesh):
    in_specs = (
        P(("groups", "ctx", "mp"), "rep"),
        P(None, "rep", "mp", None),
        P("rep"),
        P(("groups", "ctx", "mp"), "rep"),
        P(("groups", "ctx", "mp"), None),
    )
    out_specs = (P(("groups", "ctx", "mp"), "rep"), P(("groups", "ctx", "mp"), "rep"))
    return jax.shard_map(
        on_device, mesh=mesh, in_specs=in_specs, out_specs=out_specs, check_vma=False
    )
```

time: 138 us -> 41.9 us (0.30)
  blocking collectives: 35.8 us -> 0 us
  Pallas kernels: 0 us -> 34.7 us
  matrix products: 26.4 us -> 0 us
  starting transfers between devices: 21.7 us -> 0 us
  local copies, waits for them, and re-layouts: 22.3 us -> 6.24 us
  between operations: 15 us -> 0.65 us
  other arithmetic: 10.5 us -> 0 us
  waiting for transfers between devices: 5.08 us -> 0 us
    all_gather x4 -> x0, blocking collectives: 35.8 us -> none  [the longest x2 26.6 us: entering(): everything = jax.tree.map(lambda part: lax.all_gather(part, axis), x)]
    pallas_call x0 -> x1, Pallas kernels: none -> 34.7 us  [on_device(): pl.pallas_call(functools.partial(kernel, (G, C, M)), out_shape=(jax.Shape...]
    ppermute x7 -> x0, starting transfers between devices: 21.7 us -> none  [from_behind(): return lax.ppermute(x, axis, pairs)]
    dot_general x5 -> x0, matrix products: 13.4 us -> none  [the longest x4 11.1 us: attend_pair(): jnp.einsum('htk,kd->thd', probabilities, value_rows, preferred_element_ty...]
    sub x4 -> x0, matrix products: 13.1 us -> none  [attend_pair(): expd = jnp.exp(scores - row_max)]
    pad x24 -> x0, local copies, waits for them, and re-layouts: 7.74 us -> none  [on_device(): lax.associative_scan(pair_combine, (decays, driven), axis=0)]
    slice x45 -> x0, local copies, waits for them, and re-layouts: 6 us -> none  [the longest x44 5.93 us: on_device(): lax.associative_scan(pair_combine, (decays, driven), axis=0)]
    ppermute x7 -> x0, waiting for transfers between devices: 5.06 us -> none  [from_behind(): return lax.ppermute(x, axis, pairs)]
  transfers between devices with their start and end apart: 8 -> 0, of which waited for: 2 -> 0; matrix products, arithmetic and copies ran while one was open for 23% -> 0% of each run, Pallas kernels for 0% -> 0%
where the time goes in v1:
time: 41.9 us; the launch traced here: 41.6 us
  Pallas kernels  34.7 us (83%)
  local copies, waits for them, and re-layouts  6.24 us (15%)
  between operations  0.65 us (2%)
    pallas_call x1, Pallas kernels, on_device(): pl.pallas_call(functools.partial(kernel, (G, C, M)), out_shape=(jax.Shape...  34.7 us
    unnamed x12, local copies, waits for them, and re-layouts  6.24 us

profile of v1, /device:TPU:0, one launch (start us, length us, event | category | flops | bytes accessed | tf_op | source)
XLA Modules:
  0.0 41.6 jit_solution(1294368373348548043)
XLA Ops:
  0.6 0.0 copy-start
  0.6 1.2 %copy-done = bf16[2,8,128,256]{3,2,1,0:T(8,128)(2,1)S(1)} copy-done((bf16[2,8,128,256]{3,2,1,0:T(8,128)(2,1)S(1)}, bf16[2,8,128,256]{3,2,1,0:T(8,128)(2,1)}, u32[]{:S(2)}) %copy-start) | copy-done | bytes 1048600
  1.9 0.0 copy-start.1
  1.9 1.0 %copy-done.1 = bf16[128,2048]{1,0:T(8,128)(2,1)S(1)} copy-done((bf16[128,2048]{1,0:T(8,128)(2,1)S(1)}, bf16[128,2048]{1,0:T(8,128)(2,1)}, u32[]{:S(2)}) %copy-start.1) | copy-done | bytes 524312
  2.9 0.0 copy-start.2
  2.9 0.9 %copy-done.2 = bf16[128,1024]{1,0:T(8,128)(2,1)S(1)} copy-done((bf16[128,1024]{1,0:T(8,128)(2,1)S(1)}, bf16[128,1024]{1,0:T(8,128)(2,1)}, u32[]{:S(2)}) %copy-start.2) | copy-done | bytes 262168
  3.8 0.0 copy-start.3
  3.9 0.8 %copy-done.3 = bf16[128,256]{1,0:T(8,128)(2,1)S(1)} copy-done((bf16[128,256]{1,0:T(8,128)(2,1)S(1)}, bf16[128,256]{1,0:T(8,128)(2,1)}, u32[]{:S(2)}) %copy-start.3) | copy-done | bytes 65560
  4.7 0.0 copy-start.4
  4.7 0.7 %copy-done.4 = f32[2048]{0:T(1024)S(1)} copy-done((f32[2048]{0:T(1024)S(1)}, f32[2048]{0:T(1024)}, u32[]{:S(2)}) %copy-start.4) | copy-done | bytes 8216
  5.4 34.7 %shard_map.68 = (bf16[128,2048]{1,0:T(8,128)(2,1)S(1)}, bf16[128,1024]{1,0:T(8,128)(2,1)S(1)}) custom-call(bf16[128,2048]{1,0:T(8,128)(2,1)S(1)} %copy-done.1, bf16[2,8,128,256]{3,2,1,0:T(8,128)(2,1)S(1)} %copy-done, f32[1,2048]{1,0:T(1,128)S(1)} %bitcast.1, bf16[128,1024]{1,0:T(8,128)(2,1)S(1)} %copy-done.2, bf16[128,256]{1,0:T(8,128)(2,1)S(1)} %copy-done.3), custom_call_target="tpu_custom_call" | custom-call | tf_op jit(solution)/shard_map/pallas_call | solution.py:268
  40.1 0.8 %copy.9 = bf16[128,2048]{1,0:T(8,128)(2,1)} copy(bf16[128,2048]{1,0:T(8,128)(2,1)S(1)} %get-tuple-element.4) | data formatting | bytes 1048576
  40.9 0.7 %copy.10 = bf16[128,1024]{1,0:T(8,128)(2,1)} copy(bf16[128,1024]{1,0:T(8,128)(2,1)S(1)} %get-tuple-element.5) | data formatting | bytes 524288
Async XLA Ops:
  0.6 1.2 %copy-start = (bf16[2,8,128,256]{3,2,1,0:T(8,128)(2,1)S(1)}, bf16[2,8,128,256]{3,2,1,0:T(8,128)(2,1)}, u32[]{:S(2)}) copy-start(bf16[2,8,128,256]{3,2,1,0:T(8,128)(2,1)} %w_hbm.1) | copy-start | bytes 3145732
  1.9 1.0 %copy-start.1 = (bf16[128,2048]{1,0:T(8,128)(2,1)S(1)}, bf16[128,2048]{1,0:T(8,128)(2,1)}, u32[]{:S(2)}) copy-start(bf16[128,2048]{1,0:T(8,128)(2,1)} %x_hbm.1) | copy-start | bytes 1572868
  2.9 0.9 %copy-start.2 = (bf16[128,1024]{1,0:T(8,128)(2,1)S(1)}, bf16[128,1024]{1,0:T(8,128)(2,1)}, u32[]{:S(2)}) copy-start(bf16[128,1024]{1,0:T(8,128)(2,1)} %q_hbm.1) | copy-start | bytes 786436
  3.8 0.8 %copy-start.3 = (bf16[128,256]{1,0:T(8,128)(2,1)S(1)}, bf16[128,256]{1,0:T(8,128)(2,1)}, u32[]{:S(2)}) copy-start(bf16[128,256]{1,0:T(8,128)(2,1)} %kv_hbm.1) | copy-start | bytes 196612
  4.7 0.7 %copy-start.4 = (f32[2048]{0:T(1024)S(1)}, f32[2048]{0:T(1024)}, u32[]{:S(2)}) copy-start(f32[2048]{0:T(1024)} %param.7) | copy-start | bytes 24580

commit v2 on v1

--- a/solution.py
+++ b/solution.py
@@ -19,9 +19,9 @@
     x_hbm, w_hbm, decay_ref, q_hbm, kv_hbm,
     rec_ref, att_ref,
     x_ref, wbuf, q_ref, kvbuf, bias, rate, decay_run, state_run, total, totals_in,
-    local_sem, kv_send, kv_recv, w_send, w_recv, f_send, f_recv, t_send, t_recv,
+    local_sem, kv_send, kv_recv, w_send, w_recv, f_send, f_recv, t_send, t_recv, r_send, r_recv,
 ):
-    G, C, M = sizes
+    G, C, M, R = sizes
     length = C * M
     rows, width = x_ref.shape
     blocks, bw = wbuf.shape[1], wbuf.shape[4]
@@ -53,13 +53,26 @@
     lax.fori_loop(1, length, greet, 0)
     for d in range(1, G):
         pl.semaphore_signal(barrier, inc=1, device_id=((g + d) % G, c, m, r), device_id_type=MESH)
-    pl.semaphore_wait(barrier, length - 1 + G - 1)
+    for d in range(1, R):
+        pl.semaphore_signal(barrier, inc=1, device_id=(g, c, m, (r + d) % R), device_id_type=MESH)
+    pl.semaphore_wait(barrier, length - 1 + G - 1 + R - 1)
+    part = rows // R
+    mine = pl.ds(pl.multiple_of(r * part, part), part)
 
     def kv_copy(d):
         return pltpu.make_async_remote_copy(
-            src_ref=kv_hbm, dst_ref=kvbuf.at[d],
+            src_ref=kv_hbm.at[mine], dst_ref=kvbuf.at[d, mine],
             send_sem=kv_send.at[d - 1], recv_sem=kv_recv.at[d - 1],
             device_id=at((place + d) % length), device_id_type=MESH,
+        )
+
+    def r_copy(e, d, back=0):
+        owner = (r + R - back) % R
+        piece = kvbuf.at[d, pl.ds(pl.multiple_of(owner * part, part), part)]
+        return pltpu.make_async_remote_copy(
+            src_ref=piece, dst_ref=piece,
+            send_sem=r_send.at[e - 1, d - 1], recv_sem=r_recv.at[e - 1, d - 1],
+            device_id=(g, c, m, (r + e) % R), device_id_type=MESH,
         )
 
     def w_copy(d, k):
@@ -172,12 +185,18 @@
         gates(g * share + k)
         return 0
 
-    lax.fori_loop(0, share, direct, 0)
+    lax.fori_loop(0, share // 2, direct, 0)
+    for d in range(1, slots):
+        kv_copy(d).wait_recv()
+        for e in range(1, R):
+            r_copy(e, d).start()
+    lax.fori_loop(share // 2, share, direct, 0)
 
     loads[0].wait()
     loads[3].wait()
     for d in range(1, slots):
-        kv_copy(d).wait_recv()
+        for e in range(1, R):
+            r_copy(e, d, e).wait_recv()
 
     stages = share * (G - 1)
     early = min(heads // 2, stages)
@@ -237,6 +256,8 @@
 
     for d in range(1, slots):
         kv_copy(d).wait_send()
+        for e in range(1, R):
+            r_copy(e, d).wait_send()
 
     def w_sent(k, _):
         for d in range(1, M):
@@ -255,7 +276,7 @@
 
 
 def on_device(lru_in, gate_weights, decay_param, queries, keys_values):
-    G, C, M = (lax.axis_size(n) for n in ("groups", "ctx", "mp"))
+    G, C, M, R = (lax.axis_size(n) for n in ("groups", "ctx", "mp", "rep"))
     length = C * M
     rows, width = lru_in.shape
     _, blocks, depth, bw = gate_weights.shape
@@ -263,10 +284,10 @@
     reach = min(WINDOW // rows, length - 1)
     slots = reach + 1
     dma = pltpu.SemaphoreType.DMA
-    anywhere = pl.BlockSpec(memory_space=pl.ANY)
+    anywhere = pl.BlockSpec(memory_space=pltpu.HBM)
     vmem = pl.BlockSpec(memory_space=pltpu.VMEM)
     return pl.pallas_call(
-        functools.partial(kernel, (G, C, M)),
+        functools.partial(kernel, (G, C, M, R)),
         out_shape=(
             jax.ShapeDtypeStruct(lru_in.shape, BF16),
             jax.ShapeDtypeStruct(queries.shape, BF16),
@@ -293,9 +314,11 @@
             dma((G - 1, M - 1, share)),
             dma((length - 1,)),
             dma((length - 1,)),
+            dma((R - 1, reach)),
+            dma((R - 1, reach)),
         ],
         compiler_params=pltpu.CompilerParams(
-            collective_id=0, has_side_effects=True, vmem_limit_bytes=48 * 2**20
+            collective_id=0, has_side_effects=True, vmem_limit_bytes=64 * 2**20 - 917504
         ),
     )(lru_in, gate_weights, decay_param.reshape(1, width), queries, keys_values)
 

time: 41.9 us -> 37 us (0.88)
  local copies, waits for them, and re-layouts: 6.24 us -> 2.63 us
  Pallas kernels: 34.7 us -> 33.5 us
    unnamed x12 -> x4, local copies, waits for them, and re-layouts: 6.24 us -> 2.63 us
    pallas_call x1, Pallas kernels: 34.7 us -> 33.5 us  [on_device(): pl.pallas_call(functools.partial(kernel, (G, C, M, R)), out_shape=(jax.Sh...]
where the time goes in v2:
time: 37 us; the launch traced here: 36.8 us
  Pallas kernels  33.5 us (91%)
  local copies, waits for them, and re-layouts  2.63 us (7%)
  between operations  0.65 us (2%)
    pallas_call x1, Pallas kernels, on_device(): pl.pallas_call(functools.partial(kernel, (G, C, M, R)), out_shape=(jax.Sh...  33.5 us
    unnamed x4, local copies, waits for them, and re-layouts  2.63 us

profile of v2, /device:TPU:0, one launch (start us, length us, event | category | flops | bytes accessed | tf_op | source)
XLA Modules:
  0.0 36.8 jit_solution(10162212737144703658)
XLA Ops:
  0.6 33.5 %shard_map.68 = (bf16[128,2048]{1,0:T(8,128)(2,1)}, bf16[128,1024]{1,0:T(8,128)(2,1)}) custom-call(bf16[128,2048]{1,0:T(8,128)(2,1)} %x_hbm.1, bf16[2,8,128,256]{3,2,1,0:T(8,128)(2,1)} %w_hbm.1, f32[1,2048]{1,0:T(1,128)} %bitcast.1, bf16[128,1024]{1,0:T(8,128)(2,1)} %q_hbm.1, bf16[128,256]{1,0:T(8,128)(2,1)} %kv_hbm.1), custom_call_target="tpu_custom_call" | custom-call | tf_op jit(solution)/shard_map/pallas_call | solution.py:289
  34.2 0.0 copy-start
  34.2 1.9 %copy.9 = bf16[128,2048]{1,0:T(8,128)(2,1)} copy(bf16[128,2048]{1,0:T(8,128)(2,1)} %get-tuple-element.4) | data formatting | bytes 1048576
  36.1 0.0 copy-done
  36.1 0.7 %copy.10 = bf16[128,1024]{1,0:T(8,128)(2,1)} copy(bf16[128,1024]{1,0:T(8,128)(2,1)S(1)} %copy-done) | data formatting | bytes 524288
Async XLA Ops:
  34.2 1.9 %copy-start = (bf16[128,1024]{1,0:T(8,128)(2,1)S(1)}, bf16[128,1024]{1,0:T(8,128)(2,1)}, u32[]{:S(2)}) copy-start(bf16[128,1024]{1,0:T(8,128)(2,1)} %get-tuple-element.5) | copy-start | bytes 786436

commit v3 on v2

--- a/solution.py
+++ b/solution.py
@@ -109,11 +109,9 @@
             device_id=(g, c, (m + d) % M, r), device_id_type=MESH,
         )
 
-    for d in range(1, M):
-        w_copy(d, 0).start()
     for d in range(1, slots):
         kv_copy(d).start()
-    for k in range(1, share):
+    for k in range(share):
         for d in range(1, M):
             w_copy(d, k).start()
 
@@ -186,20 +184,26 @@
         return 0
 
     lax.fori_loop(0, share // 2, direct, 0)
+
+    def direct_head(k, _):
+        head(k - share // 2)
+        return direct(k, 0)
+
     for d in range(1, slots):
         kv_copy(d).wait_recv()
         for e in range(1, R):
             r_copy(e, d).start()
-    lax.fori_loop(share // 2, share, direct, 0)
 
     loads[0].wait()
     loads[3].wait()
     for d in range(1, slots):
         for e in range(1, R):
             r_copy(e, d, e).wait_recv()
+    lax.fori_loop(share // 2, share, direct_head, 0)
+    first = share - share // 2
 
     stages = share * (G - 1)
-    early = min(heads // 2, stages)
+    early = min(heads // 2, first + stages)
 
     def early_head(h, _):
         head(h)
@@ -209,9 +213,9 @@
         def relayed(k, _, e=e):
             stage = (e - 1) * share + k
 
-            @pl.when(stage < early)
+            @pl.when(first + stage < early)
             def _():
-                head(stage)
+                head(first + stage)
 
             for d in range(1, M):
                 f_arrival(e, d, k).wait_recv()
@@ -318,7 +322,7 @@
             dma((R - 1, reach)),
         ],
         compiler_params=pltpu.CompilerParams(
-            collective_id=0, has_side_effects=True, vmem_limit_bytes=64 * 2**20 - 917504
+            collective_id=0, has_side_effects=True, vmem_limit_bytes=64 * 2**20 - 1048576
         ),
     )(lru_in, gate_weights, decay_param.reshape(1, width), queries, keys_values)
 

time: 37 us -> 37.4 us (1.011)
  Pallas kernels: 33.5 us -> 33.9 us
where the time goes in v3:
time: 37.4 us; the launch traced here: 37.2 us
  Pallas kernels  33.9 us (91%)
  local copies, waits for them, and re-layouts  2.63 us (7%)
  between operations  0.65 us (2%)
    pallas_call x1, Pallas kernels, on_device(): pl.pallas_call(functools.partial(kernel, (G, C, M, R)), out_shape=(jax.Sh...  33.9 us
    unnamed x4, local copies, waits for them, and re-layouts  2.63 us

profile of v3, /device:TPU:0, one launch (start us, length us, event | category | flops | bytes accessed | tf_op | source)
XLA Modules:
  0.0 37.2 jit_solution(4445559076008714265)
XLA Ops:
  0.6 33.9 %shard_map.68 = (bf16[128,2048]{1,0:T(8,128)(2,1)}, bf16[128,1024]{1,0:T(8,128)(2,1)}) custom-call(bf16[128,2048]{1,0:T(8,128)(2,1)} %x_hbm.1, bf16[2,8,128,256]{3,2,1,0:T(8,128)(2,1)} %w_hbm.1, f32[1,2048]{1,0:T(1,128)} %bitcast.1, bf16[128,1024]{1,0:T(8,128)(2,1)} %q_hbm.1, bf16[128,256]{1,0:T(8,128)(2,1)} %kv_hbm.1), custom_call_target="tpu_custom_call" | custom-call | tf_op jit(solution)/shard_map/pallas_call | solution.py:293
  34.5 0.0 copy-start
  34.5 1.9 %copy.9 = bf16[128,2048]{1,0:T(8,128)(2,1)} copy(bf16[128,2048]{1,0:T(8,128)(2,1)} %get-tuple-element.4) | data formatting | bytes 1048576
  36.5 0.0 copy-done
  36.5 0.7 %copy.10 = bf16[128,1024]{1,0:T(8,128)(2,1)} copy(bf16[128,1024]{1,0:T(8,128)(2,1)S(1)} %copy-done) | data formatting | bytes 524288
Async XLA Ops:
  34.5 1.9 %copy-start = (bf16[128,1024]{1,0:T(8,128)(2,1)S(1)}, bf16[128,1024]{1,0:T(8,128)(2,1)}, u32[]{:S(2)}) copy-start(bf16[128,1024]{1,0:T(8,128)(2,1)} %get-tuple-element.5) | copy-start | bytes 786436
